TPU v7x, 32 devices: a whole 2x2x4 slice. The times are simulated.
32 devices in a mesh: island: 8 (over z, x), fsdp: 4 (over y, core).
Axes of the slice: x: 2, y: 2, z: 4, core: 2. Of those that a mesh axis runs over, the one named last changes fastest.
Arguments:
- local_weights: bfloat16 [8, 4096, 512], P('island', 'fsdp'), may hold values from -6 to 6
- adam_first: bfloat16 [8, 4096, 512], P('island', 'fsdp'), may hold values from -6 to 6
- adam_second: bfloat16 [8, 4096, 512], P('island', 'fsdp'), may hold values from 0.5 to 4
- global_weights: float32 [4096, 512], P('fsdp'), may hold values from -6 to 6
- outer_momentum: float32 [4096, 512], P('fsdp'), may hold values from -3 to 3
- inputs: bfloat16 [8, 512, 4096], P('island', 'fsdp'), may hold values from -6 to 6
- key_cotangent: bfloat16 [8, 512, 512], P('island', 'fsdp'), may hold values from -24 to 24
Outputs:
- new_local: bfloat16 [8, 4096, 512], P('island', 'fsdp')
- new_first: bfloat16 [8, 4096, 512], P('island', 'fsdp')
- new_second: bfloat16 [8, 4096, 512], P('island', 'fsdp')
- new_global: float32 [4096, 512], P('fsdp')
- new_momentum: float32 [4096, 512], P('fsdp')
All inputs are finite; a program needn't handle non-finite values.
Results may differ from a plain program's by a relative error of at most 0.0065.
Values may be sent and summed in bfloat16 or wider, within the bound.
A program may use at most 64 MiB of HBM per device.

v0:
```python
import jax
import jax.numpy as jnp
from jax import lax
from jax.sharding import PartitionSpec as P

HEAD_DIM = 128
beta_one = 0.9
beta_two = 0.95
inner_rate = 0.02
weight_decay = 0.1
adam_epsilon = 1e-08
norm_epsilon = 1e-06
outer_rate = 0.7
outer_beta = 0.9
merge_weight = 0.5


def key_backward(keys, upstream):
    heads = keys.shape[1] // HEAD_DIM
    shaped = keys.reshape(keys.shape[0], heads, HEAD_DIM)
    cotan_heads = upstream.reshape(keys.shape[0], heads, HEAD_DIM)
    squares = jnp.mean(shaped * shaped, axis=-1, keepdims=True)
    inverse = lax.rsqrt(squares + norm_epsilon)
    normed = shaped * inverse
    projected = jnp.mean(cotan_heads * normed, axis=-1, keepdims=True)
    return (inverse * (cotan_heads - normed * projected)).reshape(keys.shape)


def local(
    local_weights, adam_first, adam_second, global_weights, outer_momentum, inputs, key_cotangent
):
    weights = local_weights[0]
    tokens = inputs[0]
    upstream = key_cotangent[0].astype(jnp.float32)
    scale = float(tokens.shape[1]) ** (-0.5)
    islands = lax.axis_size("island")
    summed = lax.psum(weights.astype(jnp.float32), "island")
    outer_grad = global_weights - summed / islands
    new_momentum = outer_beta * outer_momentum + outer_grad
    new_global = global_weights - outer_rate * (outer_grad + outer_beta * new_momentum)
    columns = tokens
    keys = (
        jnp.dot(
            columns,
            lax.all_gather(weights, "fsdp", axis=0, tiled=True),
            preferred_element_type=jnp.float32,
        )
        * scale
    )
    key_grad = (key_backward(keys, upstream) * scale).astype(jnp.bfloat16)
    columns = tokens
    gradient = lax.psum_scatter(
        lax.dot_general(
            columns, key_grad, (((0,), (0,)), ((), ())), preferred_element_type=jnp.float32
        ).astype(jnp.bfloat16),
        "fsdp",
        scatter_dimension=0,
        tiled=True,
    ).astype(jnp.float32)
    first_new = beta_one * adam_first[0].astype(jnp.float32) + (1.0 - beta_one) * gradient
    second_new = (
        beta_two * adam_second[0].astype(jnp.float32) + (1.0 - beta_two) * gradient * gradient
    )
    current = weights.astype(jnp.float32)
    inner = current - inner_rate * (
        first_new / (jnp.sqrt(second_new) + adam_epsilon) + weight_decay * current
    )
    merged = merge_weight * inner + (1.0 - merge_weight) * new_global
    return (
        merged.astype(jnp.bfloat16)[None],
        first_new.astype(jnp.bfloat16)[None],
        second_new.astype(jnp.bfloat16)[None],
        new_global,
        new_momentum,
    )


def solution(mesh):
    placed = (
        P("island", "fsdp", None),
        P("island", "fsdp", None),
        P("island", "fsdp", None),
        P("fsdp", None),
        P("fsdp", None),
        P("island", "fsdp", None),
        P("island", "fsdp", None),
    )
    return jax.shard_map(
        local,
        mesh=mesh,
        in_specs=placed,
        out_specs=(
            P("island", "fsdp", None),
            P("island", "fsdp", None),
            P("island", "fsdp", None),
            P("fsdp", None),
            P("fsdp", None),
        ),
        check_vma=False,
    )
```

profile of v0, /device:TPU:0, one launch (start us, length us, event | category | flops | bytes accessed | tf_op | source)
XLA Modules:
  0.0 142.2 jit_solution(9254017359627056663)
XLA Ops:
  8.0 0.0 copy-start
  8.0 0.0 all-gather.3.cloned.1.call-start
  8.1 0.7 all-gather.3.cloned.1.call-update
  8.7 0.0 all-reduce.2.cloned.1.call-start
  8.8 1.5 %copy.12 = bf16[1,1024,512]{1,2,0:T(8,128)(2,1)S(1)} copy(bf16[1,1024,512]{2,1,0:T(8,128)(2,1)} %param.7) | data formatting | bytes 2097152 | tf_op args[0]
  10.3 0.0 copy-start.3
  10.3 1.6 %bitcast_convert_fusion = f32[1024,512]{0,1:T(8,128)} fusion(bf16[1,1024,512]{1,2,0:T(8,128)(2,1)S(1)} %copy.12), kind=kLoop, calls=%fused_computation.17 | loop fusion | flops 524288 | bytes 3145728 | tf_op jit(solution)/shard_map/convert_element_type | solution.py:64
  11.9 0.0 all-reduce.2.cloned.1.call-update
  11.9 0.0 reduce-scatter.2.cloned.1.call-start
  12.0 0.0 copy-done.3
  12.0 0.1 reshape.52
  12.1 35.5 %all-gather.3.cloned.1.call-done = bf16[1,4096,512]{2,1,0:T(8,128)(2,1)} async-done(((bf16[1,1024,512]{2,1,0:T(8,128)(2,1)}), bf16[1,4096,512]{2,1,0:T(8,128)(2,1)}) %all-gather.3.cloned.1.call-update) | async-done | bytes 4194320 | tf_op jit(solution)/shard_map/all_gather | solution.py:45
  47.6 0.0 copy-done
  47.6 2.9 %fusion.7 = f32[128,512]{1,0:T(8,128)S(1)} fusion(bf16[1,4096,512]{2,1,0:T(8,128)(2,1)} %all-gather.3.cloned.1.call-done, bf16[1,128,4096]{2,1,0:T(8,128)(2,1)S(1)} %copy-done), kind=kOutput, calls=%fused_computation.14 | convolution fusion | flops 536936448 | bytes 5505024 | tf_op jit(solution)/shard_map/dot_general | solution.py:43
  50.5 0.1 reshape.50
  50.6 0.2 multiply_reduce_fusion.1
  50.8 0.4 multiply_reduce_fusion
  51.2 0.2 mul.112
  51.4 0.2 mul.107
  51.6 3.3 %fusion = bf16[4096,512]{0,1:T(8,128)(2,1)} fusion(bf16[1,128,4096]{2,1,0:T(8,128)(2,1)S(1)} %copy-done, f32[16,8,4,128]{3,2,1,0:T(4,128)S(1)} %bitcast.65, f32[128,512]{1,0:T(8,128)S(1)} %fusion.7, f32[16,8,4,128]{3,2,1,0:T(4,128)S(1)} %bitcast.66, bf16[1,128,512]{2,1,0:T(8,128)(2,1)S(1)} %copy-done.3), kind=kOutput, calls=%fused_computation.1 | convolution fusion | flops 539426816 | bytes 6160384 | tf_op jit(solution)/shard_map/dot_general | solution.py:53
  54.9 0.0 reduce-scatter.2.cloned.1.call-update
  54.9 2.9 %copy.16 = f32[1024,512]{0,1:T(8,128)} copy(f32[1024,512]{1,0:T(8,128)} %param.11) | data formatting | bytes 4194304 | tf_op args[4]
  57.8 2.9 %copy.17 = f32[1024,512]{0,1:T(8,128)} copy(f32[1024,512]{1,0:T(8,128)} %param.10) | data formatting | bytes 4194304 | tf_op args[3]
  60.7 1.5 %copy.13 = bf16[1,1024,512]{1,2,0:T(8,128)(2,1)S(1)} copy(bf16[1,1024,512]{2,1,0:T(8,128)(2,1)} %param.8) | data formatting | bytes 2097152 | tf_op args[1]
  62.3 2.5 %copy.14 = bf16[1,1024,512]{1,2,0:T(8,128)(2,1)} copy(bf16[1,1024,512]{2,1,0:T(8,128)(2,1)} %param.9) | data formatting | bytes 2097152 | tf_op args[2]
  64.8 52.7 %all-reduce.2.cloned.1.call-done = f32[1024,512]{0,1:T(8,128)} async-done(((f32[1024,512]{0,1:T(8,128)}), f32[1024,512]{0,1:T(8,128)}) %all-reduce.2.cloned.1.call-update) | async-done | bytes 2097168 | tf_op jit(solution)/shard_map/psum | solution.py:37
  117.5 0.0 reduce-scatter.2.cloned.1.call-done
  117.5 6.4 %fusion.14 = (bf16[1,1024,512]{1,2,0:T(8,128)(2,1)}, f32[1024,512]{0,1:T(8,128)}, f32[1024,512]{0,1:T(8,128)}, bf16[1,1024,512]{1,2,0:T(8,128)(2,1)}, bf16[1,1024,512]{1,2,0:T(8,128)(2,1)}) fusion(bf16[1,1024,512]{1,2,0:T(8,128)(2,1)} %copy.14, bf16[1024,512]{0,1:T(8,128)(2,1)} %reduce-scatter.2.cloned.1.call-done, bf16[1,1024,512]{1,2,0:T(8,128)(2,1)S(1)} %copy.13, ...), kind=kLoop, calls=%fused_computation.20 | loop fusion | flops 15728640 | bytes 17825792 | tf_op jit(solution)/shard_map/broadcast_in_dim | solution.py:70
  123.9 2.9 %copy.21 = f32[1024,512]{1,0:T(8,128)} copy(f32[1024,512]{0,1:T(8,128)} %get-tuple-element.11) | data formatting | bytes 4194304
  126.8 2.9 %copy.22 = f32[1024,512]{1,0:T(8,128)} copy(f32[1024,512]{0,1:T(8,128)} %get-tuple-element.12) | data formatting | bytes 4194304
  129.7 0.0 copy-start.2
  129.7 0.0 copy-start.1
  129.7 2.4 %copy.18 = bf16[1,1024,512]{2,1,0:T(8,128)(2,1)} copy(bf16[1,1024,512]{1,2,0:T(8,128)(2,1)} %get-tuple-element.10) | data formatting | bytes 2097152
  132.1 0.0 copy-done.2
  132.1 1.3 copy.19
  133.4 0.0 copy-done.1
  133.4 1.3 copy.20
  (2 shorter events, 0.0 us)
Async XLA Ops:
  8.0 39.6 %copy-start = (bf16[1,128,4096]{2,1,0:T(8,128)(2,1)S(1)}, bf16[1,128,4096]{2,1,0:T(8,128)(2,1)}, u32[]{:S(2)}) copy-start(bf16[1,128,4096]{2,1,0:T(8,128)(2,1)} %param.12) | copy-start | bytes 3145732
  8.0 39.6 %all-gather.3.cloned.1.call-start = ((), (), s32[]{:S(2)}) async-start(), calls=%async_computation.3 | async-start | bytes 5242880 | tf_op jit(solution)/shard_map/all_gather | solution.py:45
  8.7 108.8 %all-reduce.2.cloned.1.call-start = ((), (), s32[]{:S(2)}) async-start(), calls=%async_computation.2 | async-start | bytes 4194304 | tf_op jit(solution)/shard_map/psum | solution.py:37
  10.3 1.7 %copy-start.3 = (bf16[1,128,512]{2,1,0:T(8,128)(2,1)S(1)}, bf16[1,128,512]{2,1,0:T(8,128)(2,1)}, u32[]{:S(2)}) copy-start(bf16[1,128,512]{2,1,0:T(8,128)(2,1)} %param.13) | copy-start | bytes 393220
  11.9 105.6 %reduce-scatter.2.cloned.1.call-start = ((), (), s32[]{:S(2)}) async-start(), calls=%async_computation.1 | async-start | bytes 5242880 | tf_op jit(solution)/shard_map/reduce_scatter | solution.py:52
  129.7 2.4 %copy-start.2 = (bf16[1,1024,512]{1,2,0:T(8,128)(2,1)S(1)}, bf16[1,1024,512]{1,2,0:T(8,128)(2,1)}, u32[]{:S(2)}) copy-start(bf16[1,1024,512]{1,2,0:T(8,128)(2,1)} %get-tuple-element.14) | copy-start | bytes 3145732
  129.7 3.7 %copy-start.1 = (bf16[1,1024,512]{1,2,0:T(8,128)(2,1)S(1)}, bf16[1,1024,512]{1,2,0:T(8,128)(2,1)}, u32[]{:S(2)}) copy-start(bf16[1,1024,512]{1,2,0:T(8,128)(2,1)} %get-tuple-element.13) | copy-start | bytes 3145732
Sparse Core Ops, SparseCore 0:
  10.4 37.1 all-gather.2
  55.0 44.4 reduce-scatter.1
Sparse Core Ops, SparseCore 1:
  12.8 104.6 all-reduce.1
where the time goes:
time: 143 us; the launch traced here: 142 us
  waiting for transfers between devices  88.9 us (62%)
  local copies, waits for them, and re-layouts  22.8 us (16%)
  between operations  15.6 us (11%)
  other arithmetic  8.62 us (6%)
  matrix products  6.16 us (4%)
    psum x1, waiting for transfers between devices, local(): summed = lax.psum(weights.astype(jnp.float32), 'island')  52.7 us
    all_gather x1, waiting for transfers between devices, local(): lax.all_gather(weights, 'fsdp', axis=0, tiled=True)  35.5 us
    unnamed x18, local copies, waits for them, and re-layouts  22.2 us
    broadcast_in_dim x1, other arithmetic, local(): merged.astype(jnp.bfloat16)[None]  6.43 us
    dot_general x1, matrix products, local(): lax.dot_general(columns, key_grad, (((0,), (0,)), ((), ())), preferred_el...  3.25 us
    dot_general x1, matrix products, local(): jnp.dot(columns, lax.all_gather(weights, 'fsdp', axis=0, tiled=True), pre...  2.9 us
  transfers between devices with their start and end apart: 3, of which 2 were waited for; matrix products, arithmetic and copies ran while one was open for 14% of the time, Pallas kernels for 0%

commit v1 on v0

--- a/solution.py
+++ b/solution.py
@@ -2,6 +2,7 @@
 import jax.numpy as jnp
 from jax import lax
 from jax.sharding import PartitionSpec as P
+from jax.lax import all_to_all, psum
 
 HEAD_DIM = 128
 beta_one = 0.9
@@ -13,6 +14,12 @@
 outer_rate = 0.7
 outer_beta = 0.9
 merge_weight = 0.5
+
+
+def launch_weights(x0, net_axis):
+    return jnp.concatenate(
+        all_to_all(jnp.stack([x0 for _ in range(psum(1, net_axis))]), net_axis, 0, 0), axis=0
+    )
 
 
 def key_backward(keys, upstream):
@@ -40,11 +47,7 @@
     new_global = global_weights - outer_rate * (outer_grad + outer_beta * new_momentum)
     columns = tokens
     keys = (
-        jnp.dot(
-            columns,
-            lax.all_gather(weights, "fsdp", axis=0, tiled=True),
-            preferred_element_type=jnp.float32,
-        )
+        jnp.dot(columns, launch_weights(weights, "fsdp"), preferred_element_type=jnp.float32)
         * scale
     )
     key_grad = (key_backward(keys, upstream) * scale).astype(jnp.bfloat16)

time: 143 us -> 152 us (1.063)
  starting transfers between devices: 0.12 us -> 5.06 us
  local copies, waits for them, and re-layouts: 22.8 us -> 25.4 us
  waiting for transfers between devices: 88.9 us -> 90.5 us
    all_to_all x0 -> x1, waiting for transfers between devices: none -> 46.6 us  [launch_weights(): all_to_all(jnp.stack([x0 for _ in range(psum(1, net_axis))]), net_axis, 0...]
    all_gather x1 -> x0, waiting for transfers between devices: 35.5 us -> none  [local(): lax.all_gather(weights, 'fsdp', axis=0, tiled=True)]
    psum x1, waiting for transfers between devices: 52.7 us -> 43.9 us  [local(): summed = lax.psum(weights.astype(jnp.float32), 'island')]
    all_to_all x0 -> x1, starting transfers between devices: none -> 4.97 us  [launch_weights(): all_to_all(jnp.stack([x0 for _ in range(psum(1, net_axis))]), net_axis, 0...]
    another operation x0 -> x1, local copies, waits for them, and re-layouts: none -> 3.62 us  [launch_weights(): jnp.stack([x0 for _ in range(psum(1, net_axis))])]
    unnamed x18 -> x20, local copies, waits for them, and re-layouts: 22.2 us -> 21.2 us
  transfers between devices with their start and end apart: 3 -> 3, of which waited for: 2 -> 2; matrix products, arithmetic and copies ran while one was open for 14% -> 13% of each run, Pallas kernels for 0% -> 0%
where the time goes in v1:
time: 152 us; the launch traced here: 151 us
  waiting for transfers between devices  90.5 us (60%)
  local copies, waits for them, and re-layouts  25.4 us (17%)
  between operations  15.6 us (10%)
  other arithmetic  8.57 us (6%)
  matrix products  6.18 us (4%)
  starting transfers between devices  5.06 us (3%)
    all_to_all x1, waiting for transfers between devices, launch_weights(): all_to_all(jnp.stack([x0 for _ in range(psum(1, net_axis))]), net_axis, 0...  46.6 us
    psum x1, waiting for transfers between devices, local(): summed = lax.psum(weights.astype(jnp.float32), 'island')  43.9 us
    unnamed x20, local copies, waits for them, and re-layouts  21.2 us
    broadcast_in_dim x1, other arithmetic, local(): merged.astype(jnp.bfloat16)[None]  6.43 us
    all_to_all x1, starting transfers between devices, launch_weights(): all_to_all(jnp.stack([x0 for _ in range(psum(1, net_axis))]), net_axis, 0...  4.97 us
    another operation x1, local copies, waits for them, and re-layouts, launch_weights(): jnp.stack([x0 for _ in range(psum(1, net_axis))])  3.62 us
    dot_general x1, matrix products, local(): lax.dot_general(columns, key_grad, (((0,), (0,)), ((), ())), preferred_el...  3.25 us
  transfers between devices with their start and end apart: 3, of which 2 were waited for; matrix products, arithmetic and copies ran while one was open for 13% of the time, Pallas kernels for 0%

profile of v1, /device:TPU:0, one launch (start us, length us, event | category | flops | bytes accessed | tf_op | source)
XLA Modules:
  0.0 151.3 jit_solution(3507645118649123327)
XLA Ops:
  8.0 0.0 copy-start
  8.0 3.6 %stack.3 = bf16[4,1024,512]{2,1,0:T(8,128)(2,1)} broadcast(bf16[1024,512]{1,0:T(8,128)(2,1)} %bitcast.62), dimensions={1,2} | broadcast | bytes 5242880 | tf_op jit(solution)/shard_map/stack | solution.py:21
  11.6 0.0 copy-start.1
  11.6 5.0 %all-to-all-start = ((bf16[4,1024,512]{2,1,0:T(8,128)(2,1)}), bf16[4,1024,512]{2,1,0:T(8,128)(2,1)}, u32[]{:S(2)}, u32[]{:S(2)}) async-start(bf16[4,1024,512]{2,1,0:T(8,128)(2,1)} %stack.3), calls=%async_computation | async-start | bytes 8388608 | tf_op jit(solution)/shard_map/all_to_all | solution.py:21
  16.6 0.0 all-reduce.2.cloned.1.call-start
  16.7 0.0 copy-done.1
  16.7 0.5 copy.12
  17.2 0.0 copy-start.4
  17.2 1.5 %bitcast_convert_fusion = f32[1024,512]{0,1:T(8,128)} fusion(bf16[1,1024,512]{1,2,0:T(8,128)(2,1)S(1)} %copy.12), kind=kLoop, calls=%fused_computation.17 | loop fusion | flops 524288 | bytes 3145728 | tf_op jit(solution)/shard_map/convert_element_type | solution.py:67
  18.8 0.0 all-reduce.2.cloned.1.call-update
  18.8 0.0 reduce-scatter.2.cloned.1.call-start
  18.8 0.0 copy-done.4
  18.9 0.1 reshape.57
  18.9 46.6 %all-to-all-done = bf16[4,1024,512]{2,1,0:T(8,128)(2,1)} async-done(((bf16[4,1024,512]{2,1,0:T(8,128)(2,1)}), bf16[4,1024,512]{2,1,0:T(8,128)(2,1)}, u32[]{:S(2)}, u32[]{:S(2)}) %all-to-all-start) | async-done | bytes 4194336 | tf_op jit(solution)/shard_map/all_to_all | solution.py:21
  65.5 0.0 copy-done
  65.5 2.9 %convolution_multiply_fusion = f32[128,512]{1,0:T(8,128)S(1)} fusion(bf16[4096,512]{1,0:T(8,128)(2,1)} %bitcast.4, bf16[1,128,4096]{2,1,0:T(8,128)(2,1)S(1)} %copy-done), kind=kOutput, calls=%fused_computation.12 | convolution fusion | flops 536936448 | bytes 5505024 | tf_op jit(solution)/shard_map/dot_general | solution.py:50
  68.4 0.1 reshape.55
  68.5 0.2 multiply_reduce_fusion.1
  68.8 0.4 multiply_reduce_fusion
  69.2 0.2 mul.112
  69.4 0.2 mul.107
  69.6 3.3 %fusion = bf16[4096,512]{0,1:T(8,128)(2,1)} fusion(bf16[1,128,4096]{2,1,0:T(8,128)(2,1)S(1)} %copy-done, f32[16,8,4,128]{3,2,1,0:T(4,128)S(1)} %bitcast.63, f32[128,512]{1,0:T(8,128)S(1)} %convolution_multiply_fusion, f32[16,8,4,128]{3,2,1,0:T(4,128)S(1)} %bitcast.64, bf16[1,128,512]{2,1,0:T(8,128)(2,1)S(1)} %copy-done.4), kind=kOutput, calls=%fused_computation.1 | convolution fusion | flops 539426816 | bytes 6160384 | tf_op jit(solution)/shard_map/dot_general | solution.py:56
  72.8 0.0 reduce-scatter.2.cloned.1.call-update
  72.8 2.9 %copy.17 = f32[1024,512]{0,1:T(8,128)} copy(f32[1024,512]{1,0:T(8,128)} %param.11) | data formatting | bytes 4194304 | tf_op args[4]
  75.7 2.9 %copy.18 = f32[1024,512]{0,1:T(8,128)} copy(f32[1024,512]{1,0:T(8,128)} %param.10) | data formatting | bytes 4194304 | tf_op args[3]
  78.6 1.7 %copy.13 = bf16[1,1024,512]{1,2,0:T(8,128)(2,1)S(1)} copy(bf16[1,1024,512]{2,1,0:T(8,128)(2,1)} %param.8) | data formatting | bytes 2097152 | tf_op args[1]
  80.4 2.3 %copy.15 = bf16[1,1024,512]{1,2,0:T(8,128)(2,1)} copy(bf16[1,1024,512]{2,1,0:T(8,128)(2,1)} %param.9) | data formatting | bytes 2097152 | tf_op args[2]
  82.6 43.9 %all-reduce.2.cloned.1.call-done = f32[1024,512]{0,1:T(8,128)} async-done(((f32[1024,512]{0,1:T(8,128)}), f32[1024,512]{0,1:T(8,128)}) %all-reduce.2.cloned.1.call-update) | async-done | bytes 2097168 | tf_op jit(solution)/shard_map/psum | solution.py:44
  126.6 0.0 reduce-scatter.2.cloned.1.call-done
  126.6 6.4 %fusion.9 = (bf16[1,1024,512]{1,2,0:T(8,128)(2,1)}, f32[1024,512]{0,1:T(8,128)}, f32[1024,512]{0,1:T(8,128)}, bf16[1,1024,512]{1,2,0:T(8,128)(2,1)}, bf16[1,1024,512]{1,2,0:T(8,128)(2,1)}) fusion(bf16[1,1024,512]{1,2,0:T(8,128)(2,1)} %copy.15, bf16[1024,512]{0,1:T(8,128)(2,1)} %reduce-scatter.2.cloned.1.call-done, bf16[1,1024,512]{1,2,0:T(8,128)(2,1)S(1)} %copy.13, ...), kind=kLoop, calls=%fused_computation.18 | loop fusion | flops 15728640 | bytes 17825792 | tf_op jit(solution)/shard_map/broadcast_in_dim | solution.py:73
  133.0 2.9 %copy.22 = f32[1024,512]{1,0:T(8,128)} copy(f32[1024,512]{0,1:T(8,128)} %get-tuple-element.11) | data formatting | bytes 4194304
  135.9 2.9 %copy.23 = f32[1024,512]{1,0:T(8,128)} copy(f32[1024,512]{0,1:T(8,128)} %get-tuple-element.12) | data formatting | bytes 4194304
  138.8 0.0 copy-start.3
  138.8 0.0 copy-start.2
  138.8 2.4 %copy.19 = bf16[1,1024,512]{2,1,0:T(8,128)(2,1)} copy(bf16[1,1024,512]{1,2,0:T(8,128)(2,1)} %get-tuple-element.10) | data formatting | bytes 2097152
  141.2 0.0 copy-done.3
  141.2 1.3 copy.20
  142.5 0.0 copy-done.2
  142.5 1.3 copy.21
  (2 shorter events, 0.0 us)
Async XLA Ops:
  8.0 57.5 %copy-start = (bf16[1,128,4096]{2,1,0:T(8,128)(2,1)S(1)}, bf16[1,128,4096]{2,1,0:T(8,128)(2,1)}, u32[]{:S(2)}) copy-start(bf16[1,128,4096]{2,1,0:T(8,128)(2,1)} %param.12) | copy-start | bytes 3145732
  11.6 5.0 %copy-start.1 = (bf16[1,1024,512]{2,1,0:T(8,128)(2,1)S(1)}, bf16[1,1024,512]{2,1,0:T(8,128)(2,1)}, u32[]{:S(2)}) copy-start(bf16[1,1024,512]{2,1,0:T(8,128)(2,1)} %param.7) | copy-start | bytes 3145732
  11.6 53.9 %all-to-all-start = ((bf16[4,1024,512]{2,1,0:T(8,128)(2,1)}), bf16[4,1024,512]{2,1,0:T(8,128)(2,1)}, u32[]{:S(2)}, u32[]{:S(2)}) async-start(bf16[4,1024,512]{2,1,0:T(8,128)(2,1)} %stack.3), calls=%async_computation | async-start | bytes 8388608 | tf_op jit(solution)/shard_map/all_to_all | solution.py:21
  16.6 110.0 %all-reduce.2.cloned.1.call-start = ((), (), s32[]{:S(2)}) async-start(), calls=%async_computation.3 | async-start | bytes 4194304 | tf_op jit(solution)/shard_map/psum | solution.py:44
  17.2 1.6 %copy-start.4 = (bf16[1,128,512]{2,1,0:T(8,128)(2,1)S(1)}, bf16[1,128,512]{2,1,0:T(8,128)(2,1)}, u32[]{:S(2)}) copy-start(bf16[1,128,512]{2,1,0:T(8,128)(2,1)} %param.13) | copy-start | bytes 393220
  18.8 107.8 %reduce-scatter.2.cloned.1.call-start = ((), (), s32[]{:S(2)}) async-start(), calls=%async_computation.2 | async-start | bytes 5242880 | tf_op jit(solution)/shard_map/reduce_scatter | solution.py:55
  138.8 2.4 %copy-start.3 = (bf16[1,1024,512]{1,2,0:T(8,128)(2,1)S(1)}, bf16[1,1024,512]{1,2,0:T(8,128)(2,1)}, u32[]{:S(2)}) copy-start(bf16[1,1024,512]{1,2,0:T(8,128)(2,1)} %get-tuple-element.14) | copy-start | bytes 3145732
  138.8 3.7 %copy-start.2 = (bf16[1,1024,512]{1,2,0:T(8,128)(2,1)S(1)}, bf16[1,1024,512]{1,2,0:T(8,128)(2,1)}, u32[]{:S(2)}) copy-start(bf16[1,1024,512]{1,2,0:T(8,128)(2,1)} %get-tuple-element.13) | copy-start | bytes 3145732
Sparse Core Ops, SparseCore 0:
  21.0 105.4 all-reduce.1
Sparse Core Ops, SparseCore 1:
  72.9 45.3 reduce-scatter.1
